TPU v7x, 512 devices: a whole 4x8x8 slice. The times are simulated.
512 devices in a mesh: sat: 16 (over z, core), seg: 32 (over y, x).
Axes of the slice: x: 4, y: 8, z: 8, core: 2. Of those that a mesh axis runs over, the one named last changes fastest.
Arguments:
- sens_params: bfloat16 [16, 32, 320, 1024], P('sat', 'seg'), may hold values from -0.59765625 to 0.59765625
- sens_state: bfloat16 [16, 32, 320, 64], P('sat', 'seg'), may hold values from -0.59765625 to 0.59765625
- misfit: float32 [16, 32, 320], P('sat', 'seg'), may hold values from -6 to 6
- depth: float32 [16, 32, 320], P('sat', 'seg'), may hold values from 0.2 to 0.9
- cycle_count: int32 [16, 32], P('sat', 'seg'), may hold values from 80 to 320, as said below
- node_side: int32 [16, 32, 320], P('sat', 'seg'), may hold values from 0 to 1, as said below
- transition: bfloat16 [16, 32, 64, 64], P('sat', 'seg'), may hold values from -0.75 to 0.75
- cont_sens: bfloat16 [16, 32, 64, 1024], P('sat', 'seg'), may hold values from -0.59765625 to 0.59765625
- noise_root: float32 [16, 32, 64, 64], P('sat', 'seg'), may hold values from -0.4 to 0.4
- cont_misfit: float32 [16, 32, 64], P('sat', 'seg'), may hold values from -6 to 6
Outputs:
- gram_params: float32 [1024, 1024], P('sat')
- grad_params: float32 [1024], replicated
- node_hess: float32 [16, 32, 64, 64], P('sat', 'seg')
- node_cross: float32 [16, 32, 64, 1024], P('sat', 'seg')
- node_grad: float32 [16, 32, 64], P('sat', 'seg')
- node_coupling: float32 [16, 32, 64, 64], P('sat', 'seg')
Inputs may be any that keep to these rules, and one draw needn't show every extreme that they name: `cycle_count`: in every segment some satellite has exactly 320 cycles. `node_side`: along the cycles of one satellite's segment the value never falls, and both values occur.
All inputs are finite; a program needn't handle non-finite values.
Results may differ from a plain program's by a relative error of at most 0.0015.
The roundings to bfloat16 on the way count: a program that leaves them out, or rounds other values in their place, can miss the bound.
Values sent between devices are 32-bit elements; how exact they have to be, the bound alone decides.
A program may use at most 64 MiB of HBM per device.

v0:
```python
import jax
import jax.numpy as jnp
from jax import lax
from jax.sharding import PartitionSpec as P

highest = lax.Precision.HIGHEST


def entering(value, axis, combine, identity):
    devices, position = (lax.axis_size(axis), lax.axis_index(axis))
    everything = lax.all_gather(value, axis)
    start = jnp.broadcast_to(jnp.asarray(identity, value.dtype), value.shape)

    def step(k, before):
        reached = k < position
        new = combine(before, everything[k])
        return jnp.where(reached, new, before)

    return lax.fori_loop(0, devices, step, start)


def passed_along(block, axis, distance):
    devices = range(lax.axis_size(axis))
    route = [(i - distance, i) for i in devices if i - distance in devices]
    return lax.ppermute(block, axis, route)


def add_pair(earlier, later):
    return earlier + later


def shards(
    sens_params,
    sens_state,
    misfit,
    depth,
    cycle_count,
    node_side,
    transition,
    cont_sens,
    noise_root,
    cont_misfit,
):
    sat_dev = sens_params.shape[0]
    cycles = sens_params.shape[2]
    params = sens_params.shape[3]
    states = sens_state.shape[3]
    sat_count = lax.axis_size("sat")
    seg_count = lax.axis_size("seg")
    seg_place = lax.axis_index("seg")
    positions = jnp.arange(cycles, dtype=jnp.int32)
    live_mask = (positions[None, :] < cycle_count).astype(jnp.float32)
    used_depth = live_mask * depth[:, 0]
    through = jnp.sum(used_depth, axis=1)
    prior_age = entering(through, "seg", add_pair, jnp.zeros_like(through))
    upper_tri = (positions[:, None] < positions[None, :]).astype(jnp.float32)
    inner_age = jnp.dot(used_depth, upper_tri, precision=highest)
    age_scale = 4.0 / (cycles * seg_count)
    weights = live_mask / (1.0 + (prior_age[:, None] + inner_age) * age_scale)
    root_seg = jnp.sqrt(weights)
    weighted_sens = (root_seg[:, :, None] * sens_params[:, 0]).astype(jnp.bfloat16)
    weighted_res = (root_seg * misfit[:, 0]).astype(jnp.bfloat16)
    side = node_side[:, 0].astype(jnp.float32)[:, :, None]
    state_rows = root_seg[:, :, None] * sens_state[:, 0]
    state_pair = jnp.concatenate([state_rows * (1.0 - side), state_rows * side], axis=2).astype(
        jnp.bfloat16
    )
    live_link = (seg_place < seg_count - 1).astype(jnp.float32)
    eye_block = jnp.eye(states, dtype=jnp.float32)
    root_info = (eye_block[None] + noise_root[:, 0]) * live_link
    state_map = jnp.einsum(
        "sab,sbc->sac", root_info, transition[:, 0].astype(jnp.float32), precision=highest
    )
    param_map = jnp.einsum(
        "sab,sbp->sap", root_info, cont_sens[:, 0].astype(jnp.float32), precision=highest
    ).astype(jnp.bfloat16)
    cont_res = jnp.einsum("sab,sb->sa", root_info, cont_misfit[:, 0], precision=highest).astype(
        jnp.bfloat16
    )
    stacked = jnp.concatenate([weighted_sens, param_map], axis=1).reshape(-1, params)
    res_vec = jnp.concatenate([weighted_res, -cont_res], axis=1).reshape(-1)
    norm_factor = 1.0 / (sat_dev * sat_count * seg_count)
    term = lax.dot_general(
        stacked, stacked, (((0,), (0,)), ((), ())), preferred_element_type=jnp.float32
    )
    row_block = lax.psum_scatter(
        term * norm_factor, ("sat", "seg"), scatter_dimension=0, tiled=True
    )
    gram_params = lax.all_gather(row_block, "seg", axis=0, tiled=True)
    grad_term = jnp.dot(res_vec, stacked, preferred_element_type=jnp.float32) * norm_factor
    grad_params = lax.psum(grad_term, ("sat", "seg"))
    pair_gram = jnp.einsum(
        "smi,smk->sik", state_pair, state_pair, preferred_element_type=jnp.float32
    )
    pair_cross = jnp.einsum(
        "smi,smp->sip", state_pair, weighted_sens, preferred_element_type=jnp.float32
    )
    pair_grad = jnp.einsum(
        "smi,sm->si", state_pair, weighted_res, preferred_element_type=jnp.float32
    )
    map_float = param_map.astype(jnp.float32)
    res_float = cont_res.astype(jnp.float32)
    own_hess = pair_gram[:, :states, :states] + jnp.einsum(
        "sai,saj->sij", state_map, state_map, precision=highest
    )
    own_cross = pair_cross[:, :states] + jnp.einsum(
        "sai,sap->sip", state_map, map_float, precision=highest
    )
    own_grad = pair_grad[:, :states] - jnp.einsum(
        "sai,sa->si", state_map, res_float, precision=highest
    )
    next_hess = pair_gram[:, states:, states:] + jnp.einsum(
        "sai,saj->sij", root_info, root_info, precision=highest
    )
    next_cross = pair_cross[:, states:] - jnp.einsum(
        "sai,sap->sip", root_info, map_float, precision=highest
    )
    next_grad = pair_grad[:, states:] + jnp.einsum(
        "sai,sa->si", root_info, res_float, precision=highest
    )
    coupling = -jnp.einsum("sai,saj->sij", state_map, root_info, precision=highest)
    got_hess, got_cross, got_grad = passed_along((next_hess, next_cross, next_grad), "seg", 1)
    node_hess = (own_hess + got_hess)[:, None]
    node_cross = (own_cross + got_cross)[:, None]
    node_grad = (own_grad + got_grad)[:, None]
    node_coupling = coupling[:, None]
    return (gram_params, grad_params, node_hess, node_cross, node_grad, node_coupling)


def solution(mesh):
    placed = (
        P("sat", "seg", None, None),
        P("sat", "seg", None, None),
        P("sat", "seg", None),
        P("sat", "seg", None),
        P("sat", "seg"),
        P("sat", "seg", None),
        P("sat", "seg", None, None),
        P("sat", "seg", None, None),
        P("sat", "seg", None, None),
        P("sat", "seg", None),
    )
    return jax.shard_map(
        shards,
        mesh=mesh,
        in_specs=placed,
        out_specs=(
            P("sat", None),
            P(),
            P("sat", "seg", None, None),
            P("sat", "seg", None, None),
            P("sat", "seg", None),
            P("sat", "seg", None, None),
        ),
        check_vma=False,
    )
```

profile of v0, /device:TPU:16, one launch (start us, length us, event | category | flops | bytes accessed | tf_op | source)
XLA Modules:
  0.0 479.6 jit_solution(1217586959932746977)
XLA Ops:
  7.9 1.3 fusion.38
  9.2 1.3 dynamic-slice
  10.5 1.4 dynamic-update-slice
  11.9 63.0 %all-reduce = f32[32]{0:T(128)S(1)} all-reduce(f32[32]{0:T(128)S(1)} %dynamic-update-slice), channel_id=1, replica_groups=mesh['sat'=16,'seg'=32] {'seg'}, use_global_device_ids=true, to_apply=%add | all-reduce | flops 32 | bytes 256
  74.8 40.4 %while.13 = (s32[]{:T(128)}, f32[1]{0:T(128)}, s32[]{:T(128)}, f32[32,1]{0,1:T(1,128)S(1)}, s32[]{:T(128)}) while((s32[]{:T(128)}, f32[1]{0:T(128)}, s32[]{:T(128)}, f32[32,1]{0,1:T(1,128)S(1)}, s32[]{:T(128)}) %tuple.40), condition=%wide.region_2.3_spmd, body=%wide.region_1.2_spmd.sunk | while | flops 5 | bytes 115 | solution.py:19
  74.8 0.6 constant_dynamic-slice_fusion.2
  76.1 0.6 constant_dynamic-slice_fusion.2
  77.3 0.6 constant_dynamic-slice_fusion.2
  78.6 0.6 constant_dynamic-slice_fusion.2
  79.9 0.6 constant_dynamic-slice_fusion.2
  81.1 0.6 constant_dynamic-slice_fusion.2
  82.4 0.6 constant_dynamic-slice_fusion.2
  83.7 0.6 constant_dynamic-slice_fusion.2
  84.9 0.6 constant_dynamic-slice_fusion.2
  86.2 0.6 constant_dynamic-slice_fusion.2
  87.5 0.6 constant_dynamic-slice_fusion.2
  88.7 0.6 constant_dynamic-slice_fusion.2
  90.0 0.6 constant_dynamic-slice_fusion.2
  91.2 0.6 constant_dynamic-slice_fusion.2
  92.5 0.6 constant_dynamic-slice_fusion.2
  93.8 0.6 constant_dynamic-slice_fusion.2
  95.0 0.6 constant_dynamic-slice_fusion.2
  96.3 0.6 constant_dynamic-slice_fusion.2
  97.6 0.6 constant_dynamic-slice_fusion.2
  98.8 0.6 constant_dynamic-slice_fusion.2
  100.1 0.6 constant_dynamic-slice_fusion.2
  101.3 0.6 constant_dynamic-slice_fusion.2
  102.6 0.6 constant_dynamic-slice_fusion.2
  103.9 0.6 constant_dynamic-slice_fusion.2
  105.1 0.6 constant_dynamic-slice_fusion.2
  106.4 0.6 constant_dynamic-slice_fusion.2
  107.7 0.6 constant_dynamic-slice_fusion.2
  108.9 0.6 constant_dynamic-slice_fusion.2
  110.2 0.6 constant_dynamic-slice_fusion.2
  111.5 0.6 constant_dynamic-slice_fusion.2
  112.7 0.6 constant_dynamic-slice_fusion.2
  114.0 0.6 constant_dynamic-slice_fusion.2
  115.2 0.7 convert_reduce_fusion
  115.9 0.7 reduce.1
  116.6 0.7 reduce.3
  117.4 0.2 convolution_reduce_fusion
  117.6 1.3 fusion.1
  118.9 0.3 convolution_convert_fusion
  119.2 3.3 convolution_multiply_fusion
  122.4 0.6 copy-done.5
  123.1 0.1 fusion.13
  123.5 3.7 collective-permute-start.2
  127.2 0.2 convolution_bitcast_fusion.3
  127.4 0.2 fusion.12
  127.6 3.1 collective-permute-start
  130.8 0.4 convolution_bitcast_fusion
  131.2 0.3 fusion.7
  131.5 4.6 collective-permute-start.1
  136.1 0.2 fusion.18
  136.3 0.1 fusion.28
  136.5 0.9 fusion.8
  137.3 110.4 %psum.7 = f32[1024]{0:T(1024)} all-reduce(f32[1024]{0:T(1024)S(1)} %broadcast_multiply_fusion), channel_id=1, replica_groups=mesh['sat'=16,'seg'=32] {'sat','seg'}, use_global_device_ids=true, to_apply=%region_4.5 | all-reduce | flops 1024 | bytes 8192 | tf_op jit(solution)/shard_map/psum | solution.py:91
  247.8 0.7 fusion.15
  248.4 0.9 fusion.11
  249.3 1.0 fusion.6
  250.3 171.4 %all-reduce.4.cloned.1.call-done = f32[1024,1024]{1,0:T(8,128)} async-done(((f32[1024,1024]{1,0:T(8,128)}), f32[1024,1024]{1,0:T(8,128)}) %all-reduce.4.cloned.1.call-update) | async-done | bytes 4194320
  421.8 0.8 dynamic-slice_bitcast_fusion
  422.5 49.4 %all-gather = f32[32,2,1024]{2,1,0:T(2,128)S(1)} all-gather(f32[1,2,1024]{2,1,0:T(2,128)S(1)} %dynamic-slice_bitcast_fusion), channel_id=1, replica_groups=mesh['sat'=16,'seg'=32] {'seg'}, dimensions={0}, use_global_device_ids=true | all-gather | bytes 270336 | tf_op jit(solution)/shard_map/all_gather | solution.py:89
  471.9 0.9 reshape.312
  (27 shorter events, 0.4 us)
Async XLA Ops:
  7.2 111.7 %copy-start = (bf16[1,1,64,1024]{3,2,1,0:T(8,128)(2,1)S(1)}, bf16[1,1,64,1024]{3,2,1,0:T(8,128)(2,1)}, u32[]{:S(2)}) copy-start(bf16[1,1,64,1024]{3,2,1,0:T(8,128)(2,1)} %param.19) | copy-start | bytes 393220
  7.2 111.7 %copy-start.2 = (f32[1,1,64,64]{3,2,1,0:T(8,128)S(1)}, f32[1,1,64,64]{3,2,1,0:T(8,128)}, u32[]{:S(2)}) copy-start(f32[1,1,64,64]{3,2,1,0:T(8,128)} %param.20) | copy-start | bytes 49156
  7.2 414.6 %all-reduce.4.cloned.1.call-start = ((), (), s32[]{:S(2)}) async-start(), calls=%async_computation | async-start | bytes 8388608
  122.4 0.7 copy-start.5
  122.4 0.8 copy-start.3
  122.4 8.4 %copy-start.1 = (bf16[1,1,320,1024]{3,2,1,0:T(8,128)(2,1)S(1)}, bf16[1,1,320,1024]{3,2,1,0:T(8,128)(2,1)}, u32[]{:S(2)}) copy-start(bf16[1,1,320,1024]{3,2,1,0:T(8,128)(2,1)} %param.12) | copy-start | bytes 1966084
  123.5 124.3 %collective-permute-start.2 = (f32[1,64]{1,0:T(1,128)S(1)}, f32[1,64]{1,0:T(1,128)S(1)}, u32[]{:S(2)}, u32[]{:S(2)}) collective-permute-start(f32[1,64]{1,0:T(1,128)S(1)} %convolution_add_fusion), channel_id=1, source_target_pairs={{0,1},{1,2},{2,3},{3,4},{4,5},{5,6},{6,7},{7,8},{8,9},{9,10},{10,1... | collective-permute-start | bytes 776 | tf_op jit(solution)/shard_map/ppermute | solution.py:25
  127.6 8.7 %copy-start.4 = (bf16[1,1,64,64]{3,2,1,0:T(8,128)(2,1)S(1)}, bf16[1,1,64,64]{3,2,1,0:T(8,128)(2,1)}, u32[]{:S(2)}) copy-start(bf16[1,1,64,64]{3,2,1,0:T(8,128)(2,1)} %param.18) | copy-start | bytes 24580
  127.6 120.8 %collective-permute-start = (f32[1,64,64]{2,1,0:T(8,128)S(1)}, f32[1,64,64]{2,1,0:T(8,128)S(1)}, u32[]{:S(2)}, u32[]{:S(2)}) collective-permute-start(f32[1,64,64]{2,1,0:T(8,128)S(1)} %fusion.12), channel_id=1, source_target_pairs={{0,1},{1,2},{2,3},{3,4},{4,5},{5,6},{6,7},{7,8},{8,9},{9,10},{10,1... | collective-permute-start | bytes 49160 | tf_op jit(solution)/shard_map/ppermute | solution.py:25
  131.5 117.8 %collective-permute-start.1 = (f32[1,64,1024]{2,1,0:T(8,128)S(1)}, f32[1,64,1024]{2,1,0:T(8,128)S(1)}, u32[]{:S(2)}, u32[]{:S(2)}) collective-permute-start(f32[1,64,1024]{2,1,0:T(8,128)S(1)} %fusion.7), channel_id=1, source_target_pairs={{0,1},{1,2},{2,3},{3,4},{4,5},{5,6},{6,7},{7,8},{8,9},{9,10},{10,1... | collective-permute-start | bytes 786440 | tf_op jit(solution)/shard_map/ppermute | solution.py:25
Sparse Core Ops, SparseCore 0:
  122.6 299.1 all-reduce.3
where the time goes:
time: 481 us; the launch traced here: 480 us
  blocking collectives  223 us (46%)
  waiting for transfers between devices  171 us (36%)
  local copies, waits for them, and re-layouts  23.7 us (5%)
  loops' own time  21.7 us (5%)
  between operations  14.9 us (3%)
  starting transfers between devices  11.4 us (2%)
  matrix products  9.03 us (2%)
    unnamed x2, waiting for transfers between devices  171 us
    psum x1, blocking collectives, shards(): grad_params = lax.psum(grad_term, ('sat', 'seg'))  110 us
    unnamed x1, blocking collectives  63 us
    all_gather x1, blocking collectives, shards(): gram_params = lax.all_gather(row_block, 'seg', axis=0, tiled=True)  49.4 us
    another operation x1, loops' own time, entering(): return lax.fori_loop(0, devices, step, start)  21.7 us
    dynamic_slice x32, local copies, waits for them, and re-layouts, step(): new = combine(before, everything[k])  18.7 us
    ppermute x3, starting transfers between devices, passed_along(): return lax.ppermute(block, axis, route)  11.3 us
  transfers between devices with their start and end apart: 4, of which 1 were waited for; matrix products, arithmetic and copies ran while one was open for 1% of the time, Pallas kernels for 0%

commit v1 on v0

--- a/solution.py
+++ b/solution.py
@@ -88,7 +88,7 @@
     )
     gram_params = lax.all_gather(row_block, "seg", axis=0, tiled=True)
     grad_term = jnp.dot(res_vec, stacked, preferred_element_type=jnp.float32) * norm_factor
-    grad_params = lax.psum(grad_term, ("sat", "seg"))
+    grad_params = jnp.sum(lax.all_gather(grad_term, ("sat", "seg")), axis=0)
     pair_gram = jnp.einsum(
         "smi,smk->sik", state_pair, state_pair, preferred_element_type=jnp.float32
     )

time: 481 us -> 551 us (1.15)
  the two profiles are of different devices: /device:TPU:16 before, /device:TPU:1 now
where the time goes in v1:
time: 551 us; the launch traced here: 550 us
  waiting for transfers between devices  369 us (67%)
  blocking collectives  99.3 us (18%)
  local copies, waits for them, and re-layouts  25.3 us (5%)
  loops' own time  21.7 us (4%)
  between operations  14.9 us (3%)
  matrix products  9.03 us (2%)
  other arithmetic  6.05 us (1%)
    unnamed x3, waiting for transfers between devices  290 us
    all_gather x1, waiting for transfers between devices, shards(): grad_params = jnp.sum(lax.all_gather(grad_term, ('sat', 'seg')), axis=0)  78.8 us
    unnamed x1, blocking collectives  61.9 us
    all_gather x1, blocking collectives, shards(): gram_params = lax.all_gather(row_block, 'seg', axis=0, tiled=True)  37.4 us
    another operation x1, loops' own time, entering(): return lax.fori_loop(0, devices, step, start)  21.7 us
    dynamic_slice x32, local copies, waits for them, and re-layouts, step(): new = combine(before, everything[k])  18.7 us
  transfers between devices with their start and end apart: 5, of which 3 were waited for; matrix products, arithmetic and copies ran while one was open for 1% of the time, Pallas kernels for 0%

profile of v1, /device:TPU:1, one launch (start us, length us, event | category | flops | bytes accessed | tf_op | source)
XLA Modules:
  0.0 549.8 jit_solution(7295292255298978156)
XLA Ops:
  7.9 1.3 fusion.38
  9.2 1.3 dynamic-slice
  10.5 1.4 dynamic-update-slice
  11.9 61.9 %all-reduce = f32[32]{0:T(128)S(1)} all-reduce(f32[32]{0:T(128)S(1)} %dynamic-update-slice), channel_id=1, replica_groups=mesh['sat'=16,'seg'=32] {'seg'}, use_global_device_ids=true, to_apply=%add | all-reduce | flops 32 | bytes 256
  73.8 40.4 %while.13 = (s32[]{:T(128)}, f32[1]{0:T(128)}, s32[]{:T(128)}, f32[32,1]{0,1:T(1,128)S(1)}, s32[]{:T(128)}) while((s32[]{:T(128)}, f32[1]{0:T(128)}, s32[]{:T(128)}, f32[32,1]{0,1:T(1,128)S(1)}, s32[]{:T(128)}) %tuple.42), condition=%wide.region_2.3_spmd, body=%wide.region_1.2_spmd.sunk | while | flops 5 | bytes 115 | solution.py:19
  73.8 0.6 constant_dynamic-slice_fusion.2
  75.0 0.6 constant_dynamic-slice_fusion.2
  76.3 0.6 constant_dynamic-slice_fusion.2
  77.5 0.6 constant_dynamic-slice_fusion.2
  78.8 0.6 constant_dynamic-slice_fusion.2
  80.1 0.6 constant_dynamic-slice_fusion.2
  81.3 0.6 constant_dynamic-slice_fusion.2
  82.6 0.6 constant_dynamic-slice_fusion.2
  83.9 0.6 constant_dynamic-slice_fusion.2
  85.1 0.6 constant_dynamic-slice_fusion.2
  86.4 0.6 constant_dynamic-slice_fusion.2
  87.6 0.6 constant_dynamic-slice_fusion.2
  88.9 0.6 constant_dynamic-slice_fusion.2
  90.2 0.6 constant_dynamic-slice_fusion.2
  91.4 0.6 constant_dynamic-slice_fusion.2
  92.7 0.6 constant_dynamic-slice_fusion.2
  94.0 0.6 constant_dynamic-slice_fusion.2
  95.2 0.6 constant_dynamic-slice_fusion.2
  96.5 0.6 constant_dynamic-slice_fusion.2
  97.8 0.6 constant_dynamic-slice_fusion.2
  99.0 0.6 constant_dynamic-slice_fusion.2
  100.3 0.6 constant_dynamic-slice_fusion.2
  101.5 0.6 constant_dynamic-slice_fusion.2
  102.8 0.6 constant_dynamic-slice_fusion.2
  104.1 0.6 constant_dynamic-slice_fusion.2
  105.3 0.6 constant_dynamic-slice_fusion.2
  106.6 0.6 constant_dynamic-slice_fusion.2
  107.9 0.6 constant_dynamic-slice_fusion.2
  109.1 0.6 constant_dynamic-slice_fusion.2
  110.4 0.6 constant_dynamic-slice_fusion.2
  111.6 0.6 constant_dynamic-slice_fusion.2
  112.9 0.6 constant_dynamic-slice_fusion.2
  114.2 0.7 convert_reduce_fusion
  114.9 0.7 reduce.1
  115.6 0.7 reduce.3
  116.5 1.3 fusion.1
  117.8 0.2 convolution_convert_fusion
  118.1 3.3 convolution_multiply_fusion
  121.4 0.6 copy-done.5
  122.2 0.3 fusion.18
  122.4 0.6 broadcast_multiply_fusion
  123.3 1.3 collective-permute-start.2
  124.9 0.2 fusion.12
  125.1 1.3 collective-permute-start
  126.4 0.4 convolution_bitcast_fusion
  126.8 0.3 fusion.7
  127.2 1.3 collective-permute-start.1
  128.7 0.9 fusion.8
  129.5 0.7 fusion.15
  130.2 0.9 fusion.11
  131.0 0.8 collective-permute-done.1
  131.8 1.0 fusion.6
  132.8 289.9 %all-reduce.4.cloned.1.call-done = f32[1024,1024]{1,0:T(8,128)} async-done(((f32[1024,1024]{1,0:T(8,128)}), f32[1024,1024]{1,0:T(8,128)}) %all-reduce.4.cloned.1.call-update) | async-done | bytes 4194320
  422.7 0.8 dynamic-slice_bitcast_fusion
  423.4 37.4 %all-gather.1 = f32[32,2,1024]{2,1,0:T(2,128)S(1)} all-gather(f32[1,2,1024]{2,1,0:T(2,128)S(1)} %dynamic-slice_bitcast_fusion), channel_id=1, replica_groups=mesh['sat'=16,'seg'=32] {'seg'}, dimensions={0}, use_global_device_ids=true | all-gather | bytes 270336 | tf_op jit(solution)/shard_map/all_gather | solution.py:89
  460.8 0.9 reshape.313
  461.7 78.8 %all-gather.4.cloned.1.call-done = f32[524288]{0:T(1024)} async-done(((f32[1024]{0:T(1024)}), f32[524288]{0:T(1024)}) %all-gather.4.cloned.1.call-update) | async-done | bytes 2097168 | tf_op jit(solution)/shard_map/all_gather | solution.py:91
  540.5 1.7 reshape.308
  542.2 0.7 reduce_sum.19
  (31 shorter events, 1.1 us)
Async XLA Ops:
  7.2 110.6 %copy-start = (bf16[1,1,64,1024]{3,2,1,0:T(8,128)(2,1)S(1)}, bf16[1,1,64,1024]{3,2,1,0:T(8,128)(2,1)}, u32[]{:S(2)}) copy-start(bf16[1,1,64,1024]{3,2,1,0:T(8,128)(2,1)} %param.19) | copy-start | bytes 393220
  7.2 110.6 %copy-start.2 = (f32[1,1,64,64]{3,2,1,0:T(8,128)S(1)}, f32[1,1,64,64]{3,2,1,0:T(8,128)}, u32[]{:S(2)}) copy-start(f32[1,1,64,64]{3,2,1,0:T(8,128)} %param.20) | copy-start | bytes 49156
  7.2 415.5 %all-reduce.4.cloned.1.call-start = ((), (), s32[]{:S(2)}) async-start(), calls=%async_computation.1 | async-start | bytes 8388608
  121.3 0.7 copy-start.5
  121.3 1.7 copy-start.3
  121.4 5.1 copy-start.1
  121.4 419.1 %all-gather.4.cloned.1.call-start = ((), (), s32[]{:S(2)}) async-start(), calls=%async_computation | async-start | bytes 2101248 | tf_op jit(solution)/shard_map/all_gather | solution.py:91
  122.4 6.1 %copy-start.4 = (bf16[1,1,64,64]{3,2,1,0:T(8,128)(2,1)S(1)}, bf16[1,1,64,64]{3,2,1,0:T(8,128)(2,1)}, u32[]{:S(2)}) copy-start(bf16[1,1,64,64]{3,2,1,0:T(8,128)(2,1)} %param.18) | copy-start | bytes 24580
  123.3 6.2 %collective-permute-start.2 = (f32[1,64]{1,0:T(1,128)S(1)}, f32[1,64]{1,0:T(1,128)S(1)}, u32[]{:S(2)}, u32[]{:S(2)}) collective-permute-start(f32[1,64]{1,0:T(1,128)S(1)} %convolution_add_fusion), channel_id=1, source_target_pairs={{0,1},{1,2},{2,3},{3,4},{4,5},{5,6},{6,7},{7,8},{8,9},{9,10},{10,1... | collective-permute-start | bytes 776 | tf_op jit(solution)/shard_map/ppermute | solution.py:25
  125.1 5.0 collective-permute-start
  127.2 4.6 collective-permute-start.1
Sparse Core Ops, SparseCore 0:
  121.5 301.1 all-reduce.3
  427.4 113.0 all-gather.3
